TPU v7x, 32 devices: a whole 2x2x4 slice. The times are simulated.
32 devices in a mesh: tm: 4 (over z), space: 8 (over y, x, core).
Axes of the slice: x: 2, y: 2, z: 4, core: 2. Of those that a mesh axis runs over, the one named last changes fastest.
Arguments:
- c_state: float32 [4, 2, 64, 2048], P('tm', None, 'space'), may hold values from -4 to 4
Outputs:
- next_state: float32 [4, 2, 64, 2048], P('tm', None, 'space')
All inputs are finite; a program needn't handle non-finite values.
Results may differ from a plain program's by a relative error of at most 0.00002.
Values sent between devices are 32-bit elements; how exact they have to be, the bound alone decides.
No kernel may reach another device: no remote copies, remote signals or barrier semaphores. Data moves between devices by JAX's collectives and lax.ppermute only.
A program may use at most 64 MiB of HBM per device.

v0:
```python
import jax
import jax.numpy as jnp
from jax import lax
from jax.sharding import PartitionSpec as P

FSTEPS = 4
CF = 4
COURANT = 0.06
DIFFUSION = 0.04


def padded_2(block, sides, width):
    for axis, dim in sides:
        count = lax.axis_size(axis)
        forward = [(i, i + 1) for i in range(count - 1)]
        forward.append((count - 1, 0))
        backward = [(target, source) for source, target in forward]
        low = lax.ppermute(
            lax.slice_in_dim(block, block.shape[dim] - width, None, axis=dim), axis, forward
        )
        high = lax.ppermute(lax.slice_in_dim(block, 0, width, axis=dim), axis, backward)
        block = jnp.concatenate([low, block, high], axis=dim)
    return block


def advance(padded, courant, diffusion):
    center = padded[:, 1:-1]
    row_above = padded[:, :-2]
    row_below = padded[:, 2:]
    col_left = jnp.roll(center, 1, axis=2)
    col_right = jnp.roll(center, -1, axis=2)
    along_u = center[0:1]
    along_v = center[1:2]
    transport = jnp.maximum(along_u, 0.0) * (center - row_above) + jnp.minimum(along_u, 0.0) * (
        row_below - center
    )
    transport = (
        transport
        + jnp.maximum(along_v, 0.0) * (center - col_left)
        + jnp.minimum(along_v, 0.0) * (col_right - center)
    )
    spread = row_above + row_below + col_left + col_right - 4.0 * center
    return center - courant * transport + diffusion * spread


def restrict(field):
    blocks = field.reshape(field.shape[0], field.shape[1] // CF, CF, field.shape[2] // CF, CF)
    return jnp.mean(blocks, axis=(2, 4))


def prolong(field):
    return jnp.repeat(jnp.repeat(field, CF, axis=1), CF, axis=2)


def coarse_step(field):
    padded = padded_2(field, (("space", 1),), 1)
    return advance(padded, COURANT * FSTEPS / CF, DIFFUSION * FSTEPS / (CF * CF))


def body(c_state):
    field = c_state[0]
    for section_index in range(FSTEPS):
        padded = padded_2(field, (("space", 1),), 1)
        field = advance(padded, COURANT, DIFFUSION)
    start_coarse = restrict(c_state[0])
    end_coarse = restrict(field)
    defect = end_coarse - coarse_step(start_coarse)
    group_index = lax.axis_index("tm")
    all_start, all_defect = (
        lax.all_gather(start_coarse[None], "tm", axis=0, tiled=True),
        lax.all_gather(defect[None], "tm", axis=0, tiled=True),
    )

    def chain_step(carry, defect_term):
        advanced = coarse_step(carry) + defect_term
        return (advanced, advanced)

    unused, coarse_path = lax.scan(chain_step, all_start[0], all_defect)
    reached = lax.dynamic_index_in_dim(coarse_path, group_index, 0, keepdims=False)
    next_state = field + prolong(reached - end_coarse)
    return next_state[None]


def solution(mesh):
    placed = (P("tm", None, "space", None),)
    return jax.shard_map(
        body, mesh=mesh, in_specs=placed, out_specs=P("tm", None, "space", None), check_vma=False
    )
```

profile of v0, /device:TPU:0, one launch (start us, length us, event | category | flops | bytes accessed | tf_op | source)
XLA Modules:
  0.0 84.8 jit_solution(13688418001067768919)
XLA Ops:
  0.0 1.0 %fusion.74 = (f32[2,1,2048]{2,1,0:T(1,128)S(1)}, f32[2,1,2048]{2,1,0:T(1,128)S(1)}) fusion(f32[2,8,2048]{2,1,0:T(8,128)} %bitcast.68), kind=kLoop, calls=%fused_computation.128 | loop fusion | bytes 65536 | tf_op jit(solution)/shard_map/slice | solution.py:19
  1.6 2.9 %collective-permute-start.3 = (f32[2,1,2048]{2,0,1:T(2,128)S(1)}, f32[2,1,2048]{2,0,1:T(2,128)S(1)}, u32[]{:S(2)}, u32[]{:S(2)}) collective-permute-start(f32[2,1,2048]{2,0,1:T(2,128)S(1)} %copy.154), channel_id=1, source_target_pairs={{1,0},{2,1},{3,2},{4,3},{5,4},{6,5},{7,6},{0,7},{9,8},{10,9},{11,1... | collective-permute-start | bytes 49160 | tf_op jit(solution)/shard_map/ppermute | solution.py:21
  4.5 6.5 %reshape_squeeze.3 = f32[2,2,4,512,4]{4,3,2,1,0:T(8,128)} reshape(f32[1,2,8,2048]{3,2,1,0:T(8,128)} %param.3) | data formatting | bytes 262144 | tf_op jit(solution)/shard_map/reshape;squeeze | solution.py:47
  11.0 2.5 %reduce_sum.18 = f32[2,2,512]{2,1,0:T(2,128)S(1)} reduce(f32[2,2,4,512,4]{4,3,2,1,0:T(8,128)} %reshape_squeeze.3, f32[]{:T(128)} %constant.9.clone.1), dimensions={2,4}, to_apply=%region_0.1 | reduce | flops 30720 | bytes 139268 | tf_op jit(solution)/shard_map/reduce_sum | solution.py:48
  13.7 2.6 %collective-permute-start.11 = (f32[2,1,512]{2,1,0:T(1,128)S(1)}, f32[2,1,512]{2,1,0:T(1,128)S(1)}, u32[]{:S(2)}, u32[]{:S(2)}) collective-permute-start(f32[2,1,512]{2,1,0:T(1,128)S(1)} %get-tuple-element.93), channel_id=1, source_target_pairs={{1,0},{2,1},{3,2},{4,3},{5,4},{6,5},{7,6},{0,7},{9,8},{10,9},{11,1... | collective-permute-start | bytes 12296 | tf_op jit(solution)/shard_map/ppermute | solution.py:21
  16.7 14.1 %all-gather = f32[8,2,512]{2,1,0:T(2,128)S(1)} all-gather(f32[2,2,512]{2,1,0:T(2,128)S(1)} %broadcast_multiply_fusion), channel_id=2, replica_groups=mesh['tm'=4,'space'=8] {'tm'}, dimensions={0}, use_global_device_ids=true | all-gather | bytes 40960 | tf_op jit(solution)/shard_map/all_gather | solution.py:70
  31.3 2.7 %collective-permute-start.5 = (f32[2,1,2048]{2,0,1:T(2,128)S(1)}, f32[2,1,2048]{2,0,1:T(2,128)S(1)}, u32[]{:S(2)}, u32[]{:S(2)}) collective-permute-start(f32[2,1,2048]{2,0,1:T(2,128)S(1)} %copy.158), channel_id=1, source_target_pairs={{1,0},{2,1},{3,2},{4,3},{5,4},{6,5},{7,6},{0,7},{9,8},{10,9},{11,1... | collective-permute-start | bytes 49160 | tf_op jit(solution)/shard_map/ppermute | solution.py:21
  34.0 1.3 %collective-permute-done.4 = f32[2,1,2048]{2,0,1:T(2,128)S(1)} collective-permute-done((f32[2,1,2048]{2,0,1:T(2,128)S(1)}, f32[2,1,2048]{2,0,1:T(2,128)S(1)}, u32[]{:S(2)}, u32[]{:S(2)}) %collective-permute-start.4) | collective-permute-done | bytes 16416 | tf_op jit(solution)/shard_map/ppermute | solution.py:18
  35.8 2.7 %collective-permute-start.7 = (f32[2,1,2048]{2,0,1:T(2,128)S(1)}, f32[2,1,2048]{2,0,1:T(2,128)S(1)}, u32[]{:S(2)}, u32[]{:S(2)}) collective-permute-start(f32[2,1,2048]{2,0,1:T(2,128)S(1)} %copy.162), channel_id=1, source_target_pairs={{1,0},{2,1},{3,2},{4,3},{5,4},{6,5},{7,6},{0,7},{9,8},{10,9},{11,1... | collective-permute-start | bytes 49160 | tf_op jit(solution)/shard_map/ppermute | solution.py:21
  38.6 1.3 %collective-permute-done.6 = f32[2,1,2048]{2,0,1:T(2,128)S(1)} collective-permute-done((f32[2,1,2048]{2,0,1:T(2,128)S(1)}, f32[2,1,2048]{2,0,1:T(2,128)S(1)}, u32[]{:S(2)}, u32[]{:S(2)}) %collective-permute-start.6) | collective-permute-done | bytes 16416 | tf_op jit(solution)/shard_map/ppermute | solution.py:18
  40.9 2.1 %collective-permute-start.9 = (f32[2,1,2048]{2,0,1:T(2,128)S(1)}, f32[2,1,2048]{2,0,1:T(2,128)S(1)}, u32[]{:S(2)}, u32[]{:S(2)}) collective-permute-start(f32[2,1,2048]{2,0,1:T(2,128)S(1)} %copy.166), channel_id=1, source_target_pairs={{1,0},{2,1},{3,2},{4,3},{5,4},{6,5},{7,6},{0,7},{9,8},{10,9},{11,1... | collective-permute-start | bytes 49160 | tf_op jit(solution)/shard_map/ppermute | solution.py:21
  43.1 1.3 %collective-permute-done.8 = f32[2,1,2048]{2,0,1:T(2,128)S(1)} collective-permute-done((f32[2,1,2048]{2,0,1:T(2,128)S(1)}, f32[2,1,2048]{2,0,1:T(2,128)S(1)}, u32[]{:S(2)}, u32[]{:S(2)}) %collective-permute-start.8) | collective-permute-done | bytes 16416 | tf_op jit(solution)/shard_map/ppermute | solution.py:18
  44.7 5.7 %reshape.56 = f32[2,2,4,512,4]{4,3,2,1,0:T(8,128)} reshape(f32[2,8,2048]{2,1,0:T(8,128)S(1)} %fusion.6) | data formatting | bytes 262144 | tf_op jit(solution)/shard_map/reshape | solution.py:47
  50.4 2.5 %reduce_sum.19 = f32[2,2,512]{2,1,0:T(2,128)S(1)} reduce(f32[2,2,4,512,4]{4,3,2,1,0:T(8,128)} %reshape.56, f32[]{:T(128)} %constant.9.clone.1), dimensions={2,4}, to_apply=%region_1.2 | reduce | flops 30720 | bytes 139268 | tf_op jit(solution)/shard_map/reduce_sum | solution.py:48
  53.0 13.1 %all-gather.1 = f32[8,2,512]{2,1,0:T(2,128)S(1)} all-gather(f32[2,2,512]{2,1,0:T(2,128)S(1)} %add_subtract_fusion), channel_id=3, replica_groups=mesh['tm'=4,'space'=8] {'tm'}, dimensions={0}, use_global_device_ids=true | all-gather | bytes 40960 | tf_op jit(solution)/shard_map/all_gather | solution.py:71
  66.2 16.7 %while.12 = (s32[]{:T(128)}, f32[2,2,512]{2,1,0:T(2,128)S(1)}, f32[4,2,2,512]{3,2,1,0:T(2,128)S(1)}, f32[4,2,2,512]{3,2,1,0:T(2,128)S(1)}, s32[]{:T(128)}) while((s32[]{:T(128)}, f32[2,2,512]{2,1,0:T(2,128)S(1)}, f32[4,2,2,512]{3,2,1,0:T(2,128)S(1)}, f32[4,2,2,512]{3,2,1,0:T(2,128)S(1)}, s32[]{:T(128)}) %tuple.68), condition=%wide.region_3.4_spmd, body=%wide.region_2.3_spmd.sunk | while | flops 55298 | bytes 200857 | solution.py:78
  66.9 0.7 collective-permute-done
  67.6 2.7 %collective-permute-done.1 = f32[2,1,512]{2,1,0:T(1,128)S(1)} collective-permute-done((f32[2,1,512]{2,1,0:T(1,128)S(1)}, f32[2,1,512]{2,1,0:T(1,128)S(1)}, u32[]{:S(2)}, u32[]{:S(2)}) %collective-permute-start.1) | collective-permute-done | bytes 4128 | tf_op jit(solution)/shard_map/while/body/eval_jaxpr/ppermute | solution.py:18
  71.1 0.7 collective-permute-done
  71.8 2.7 %collective-permute-done.1 = f32[2,1,512]{2,1,0:T(1,128)S(1)} collective-permute-done((f32[2,1,512]{2,1,0:T(1,128)S(1)}, f32[2,1,512]{2,1,0:T(1,128)S(1)}, u32[]{:S(2)}, u32[]{:S(2)}) %collective-permute-start.1) | collective-permute-done | bytes 4128 | tf_op jit(solution)/shard_map/while/body/eval_jaxpr/ppermute | solution.py:18
  76.0 2.7 %collective-permute-done.1 = f32[2,1,512]{2,1,0:T(1,128)S(1)} collective-permute-done((f32[2,1,512]{2,1,0:T(1,128)S(1)}, f32[2,1,512]{2,1,0:T(1,128)S(1)}, u32[]{:S(2)}, u32[]{:S(2)}) %collective-permute-start.1) | collective-permute-done | bytes 4128 | tf_op jit(solution)/shard_map/while/body/eval_jaxpr/ppermute | solution.py:18
  79.5 0.7 collective-permute-done
  80.1 2.7 %collective-permute-done.1 = f32[2,1,512]{2,1,0:T(1,128)S(1)} collective-permute-done((f32[2,1,512]{2,1,0:T(1,128)S(1)}, f32[2,1,512]{2,1,0:T(1,128)S(1)}, u32[]{:S(2)}, u32[]{:S(2)}) %collective-permute-start.1) | collective-permute-done | bytes 4128 | tf_op jit(solution)/shard_map/while/body/eval_jaxpr/ppermute | solution.py:18
  84.1 0.7 add_bitcast_fusion
  (96 shorter events, 8.5 us)
Async XLA Ops:
  1.0 29.8 %collective-permute-start.2 = (f32[2,1,2048]{2,0,1:T(2,128)S(1)}, f32[2,1,2048]{2,0,1:T(2,128)S(1)}, u32[]{:S(2)}, u32[]{:S(2)}) collective-permute-start(f32[2,1,2048]{2,0,1:T(2,128)S(1)} %copy.152), channel_id=1, source_target_pairs={{0,1},{1,2},{2,3},{3,4},{4,5},{5,6},{6,7},{7,0},{8,9},{9,10},{10,1... | collective-permute-start | bytes 49160 | tf_op jit(solution)/shard_map/ppermute | solution.py:18
  1.6 14.7 %copy-start = (f32[1,2,8,2048]{3,2,1,0:T(8,128)S(1)}, f32[1,2,8,2048]{3,2,1,0:T(8,128)}, u32[]{:S(2)}) copy-start(f32[1,2,8,2048]{3,2,1,0:T(8,128)} %param.3) | copy-start | bytes 393220
  1.6 29.2 %collective-permute-start.3 = (f32[2,1,2048]{2,0,1:T(2,128)S(1)}, f32[2,1,2048]{2,0,1:T(2,128)S(1)}, u32[]{:S(2)}, u32[]{:S(2)}) collective-permute-start(f32[2,1,2048]{2,0,1:T(2,128)S(1)} %copy.154), channel_id=1, source_target_pairs={{1,0},{2,1},{3,2},{4,3},{5,4},{6,5},{7,6},{0,7},{9,8},{10,9},{11,1... | collective-permute-start | bytes 49160 | tf_op jit(solution)/shard_map/ppermute | solution.py:21
  13.6 39.3 %collective-permute-start.10 = (f32[2,1,512]{2,1,0:T(1,128)S(1)}, f32[2,1,512]{2,1,0:T(1,128)S(1)}, u32[]{:S(2)}, u32[]{:S(2)}) collective-permute-start(f32[2,1,512]{2,1,0:T(1,128)S(1)} %get-tuple-element.92), channel_id=1, source_target_pairs={{0,1},{1,2},{2,3},{3,4},{4,5},{5,6},{6,7},{7,0},{8,9},{9,10},{10,1... | collective-permute-start | bytes 12296 | tf_op jit(solution)/shard_map/ppermute | solution.py:18
  13.7 39.3 %collective-permute-start.11 = (f32[2,1,512]{2,1,0:T(1,128)S(1)}, f32[2,1,512]{2,1,0:T(1,128)S(1)}, u32[]{:S(2)}, u32[]{:S(2)}) collective-permute-start(f32[2,1,512]{2,1,0:T(1,128)S(1)} %get-tuple-element.93), channel_id=1, source_target_pairs={{1,0},{2,1},{3,2},{4,3},{5,4},{6,5},{7,6},{0,7},{9,8},{10,9},{11,1... | collective-permute-start | bytes 12296 | tf_op jit(solution)/shard_map/ppermute | solution.py:21
  31.2 4.2 %collective-permute-start.4 = (f32[2,1,2048]{2,0,1:T(2,128)S(1)}, f32[2,1,2048]{2,0,1:T(2,128)S(1)}, u32[]{:S(2)}, u32[]{:S(2)}) collective-permute-start(f32[2,1,2048]{2,0,1:T(2,128)S(1)} %copy.156), channel_id=1, source_target_pairs={{0,1},{1,2},{2,3},{3,4},{4,5},{5,6},{6,7},{7,0},{8,9},{9,10},{10,1... | collective-permute-start | bytes 49160 | tf_op jit(solution)/shard_map/ppermute | solution.py:18
  31.3 4.1 %collective-permute-start.5 = (f32[2,1,2048]{2,0,1:T(2,128)S(1)}, f32[2,1,2048]{2,0,1:T(2,128)S(1)}, u32[]{:S(2)}, u32[]{:S(2)}) collective-permute-start(f32[2,1,2048]{2,0,1:T(2,128)S(1)} %copy.158), channel_id=1, source_target_pairs={{1,0},{2,1},{3,2},{4,3},{5,4},{6,5},{7,6},{0,7},{9,8},{10,9},{11,1... | collective-permute-start | bytes 49160 | tf_op jit(solution)/shard_map/ppermute | solution.py:21
  35.7 4.1 %collective-permute-start.6 = (f32[2,1,2048]{2,0,1:T(2,128)S(1)}, f32[2,1,2048]{2,0,1:T(2,128)S(1)}, u32[]{:S(2)}, u32[]{:S(2)}) collective-permute-start(f32[2,1,2048]{2,0,1:T(2,128)S(1)} %copy.160), channel_id=1, source_target_pairs={{0,1},{1,2},{2,3},{3,4},{4,5},{5,6},{6,7},{7,0},{8,9},{9,10},{10,1... | collective-permute-start | bytes 49160 | tf_op jit(solution)/shard_map/ppermute | solution.py:18
  35.8 4.1 %collective-permute-start.7 = (f32[2,1,2048]{2,0,1:T(2,128)S(1)}, f32[2,1,2048]{2,0,1:T(2,128)S(1)}, u32[]{:S(2)}, u32[]{:S(2)}) collective-permute-start(f32[2,1,2048]{2,0,1:T(2,128)S(1)} %copy.162), channel_id=1, source_target_pairs={{1,0},{2,1},{3,2},{4,3},{5,4},{6,5},{7,6},{0,7},{9,8},{10,9},{11,1... | collective-permute-start | bytes 49160 | tf_op jit(solution)/shard_map/ppermute | solution.py:21
  40.3 4.1 %collective-permute-start.8 = (f32[2,1,2048]{2,0,1:T(2,128)S(1)}, f32[2,1,2048]{2,0,1:T(2,128)S(1)}, u32[]{:S(2)}, u32[]{:S(2)}) collective-permute-start(f32[2,1,2048]{2,0,1:T(2,128)S(1)} %copy.164), channel_id=1, source_target_pairs={{0,1},{1,2},{2,3},{3,4},{4,5},{5,6},{6,7},{7,0},{8,9},{9,10},{10,1... | collective-permute-start | bytes 49160 | tf_op jit(solution)/shard_map/ppermute | solution.py:18
  40.9 3.6 %collective-permute-start.9 = (f32[2,1,2048]{2,0,1:T(2,128)S(1)}, f32[2,1,2048]{2,0,1:T(2,128)S(1)}, u32[]{:S(2)}, u32[]{:S(2)}) collective-permute-start(f32[2,1,2048]{2,0,1:T(2,128)S(1)} %copy.166), channel_id=1, source_target_pairs={{1,0},{2,1},{3,2},{4,3},{5,4},{6,5},{7,6},{0,7},{9,8},{10,9},{11,1... | collective-permute-start | bytes 49160 | tf_op jit(solution)/shard_map/ppermute | solution.py:21
  66.2 1.4 %collective-permute-start = (f32[2,1,512]{2,1,0:T(1,128)S(1)}, f32[2,1,512]{2,1,0:T(1,128)S(1)}, u32[]{:S(2)}, u32[]{:S(2)}) collective-permute-start(f32[2,1,512]{2,1,0:T(1,128)S(1)} %get-tuple-element.141), channel_id=1, source_target_pairs={{1,0},{2,1},{3,2},{4,3},{5,4},{6,5},{7,6},{0,7},{9,8},{10,9},{11,1... | collective-permute-start | bytes 12296 | tf_op jit(solution)/shard_map/while/body/eval_jaxpr/ppermute | solution.py:21
  66.3 4.0 %collective-permute-start.1 = (f32[2,1,512]{2,1,0:T(1,128)S(1)}, f32[2,1,512]{2,1,0:T(1,128)S(1)}, u32[]{:S(2)}, u32[]{:S(2)}) collective-permute-start(f32[2,1,512]{2,1,0:T(1,128)S(1)} %get-tuple-element.143), channel_id=1, source_target_pairs={{0,1},{1,2},{2,3},{3,4},{4,5},{5,6},{6,7},{7,0},{8,9},{9,10},{10,1... | collective-permute-start | bytes 12296 | tf_op jit(solution)/shard_map/while/body/eval_jaxpr/ppermute | solution.py:18
  70.4 1.4 %collective-permute-start = (f32[2,1,512]{2,1,0:T(1,128)S(1)}, f32[2,1,512]{2,1,0:T(1,128)S(1)}, u32[]{:S(2)}, u32[]{:S(2)}) collective-permute-start(f32[2,1,512]{2,1,0:T(1,128)S(1)} %get-tuple-element.141), channel_id=1, source_target_pairs={{1,0},{2,1},{3,2},{4,3},{5,4},{6,5},{7,6},{0,7},{9,8},{10,9},{11,1... | collective-permute-start | bytes 12296 | tf_op jit(solution)/shard_map/while/body/eval_jaxpr/ppermute | solution.py:21
  70.4 4.0 %collective-permute-start.1 = (f32[2,1,512]{2,1,0:T(1,128)S(1)}, f32[2,1,512]{2,1,0:T(1,128)S(1)}, u32[]{:S(2)}, u32[]{:S(2)}) collective-permute-start(f32[2,1,512]{2,1,0:T(1,128)S(1)} %get-tuple-element.143), channel_id=1, source_target_pairs={{0,1},{1,2},{2,3},{3,4},{4,5},{5,6},{6,7},{7,0},{8,9},{9,10},{10,1... | collective-permute-start | bytes 12296 | tf_op jit(solution)/shard_map/while/body/eval_jaxpr/ppermute | solution.py:18
  74.6 1.4 %collective-permute-start = (f32[2,1,512]{2,1,0:T(1,128)S(1)}, f32[2,1,512]{2,1,0:T(1,128)S(1)}, u32[]{:S(2)}, u32[]{:S(2)}) collective-permute-start(f32[2,1,512]{2,1,0:T(1,128)S(1)} %get-tuple-element.141), channel_id=1, source_target_pairs={{1,0},{2,1},{3,2},{4,3},{5,4},{6,5},{7,6},{0,7},{9,8},{10,9},{11,1... | collective-permute-start | bytes 12296 | tf_op jit(solution)/shard_map/while/body/eval_jaxpr/ppermute | solution.py:21
  74.6 4.0 %collective-permute-start.1 = (f32[2,1,512]{2,1,0:T(1,128)S(1)}, f32[2,1,512]{2,1,0:T(1,128)S(1)}, u32[]{:S(2)}, u32[]{:S(2)}) collective-permute-start(f32[2,1,512]{2,1,0:T(1,128)S(1)} %get-tuple-element.143), channel_id=1, source_target_pairs={{0,1},{1,2},{2,3},{3,4},{4,5},{5,6},{6,7},{7,0},{8,9},{9,10},{10,1... | collective-permute-start | bytes 12296 | tf_op jit(solution)/shard_map/while/body/eval_jaxpr/ppermute | solution.py:18
  78.8 1.4 %collective-permute-start = (f32[2,1,512]{2,1,0:T(1,128)S(1)}, f32[2,1,512]{2,1,0:T(1,128)S(1)}, u32[]{:S(2)}, u32[]{:S(2)}) collective-permute-start(f32[2,1,512]{2,1,0:T(1,128)S(1)} %get-tuple-element.141), channel_id=1, source_target_pairs={{1,0},{2,1},{3,2},{4,3},{5,4},{6,5},{7,6},{0,7},{9,8},{10,9},{11,1... | collective-permute-start | bytes 12296 | tf_op jit(solution)/shard_map/while/body/eval_jaxpr/ppermute | solution.py:21
  78.8 4.0 %collective-permute-start.1 = (f32[2,1,512]{2,1,0:T(1,128)S(1)}, f32[2,1,512]{2,1,0:T(1,128)S(1)}, u32[]{:S(2)}, u32[]{:S(2)}) collective-permute-start(f32[2,1,512]{2,1,0:T(1,128)S(1)} %get-tuple-element.143), channel_id=1, source_target_pairs={{0,1},{1,2},{2,3},{3,4},{4,5},{5,6},{6,7},{7,0},{8,9},{9,10},{10,1... | collective-permute-start | bytes 12296 | tf_op jit(solution)/shard_map/while/body/eval_jaxpr/ppermute | solution.py:18
where the time goes:
time: 85.1 us; the launch traced here: 84.8 us
  blocking collectives  27.3 us (32%)
  waiting for transfers between devices  17.4 us (20%)
  starting transfers between devices  16.6 us (20%)
  local copies, waits for them, and re-layouts  16 us (19%)
  other arithmetic  7.04 us (8%)
    ppermute x9, waiting for transfers between devices, padded_2(): lax.ppermute(lax.slice_in_dim(block, block.shape[dim] - width, None, axis...  14.6 us
    all_gather x1, blocking collectives, body(): lax.all_gather(start_coarse[None], 'tm', axis=0, tiled=True)  14.1 us
    ppermute x9, starting transfers between devices, padded_2(): lax.ppermute(lax.slice_in_dim(block, 0, width, axis=dim), axis, backward)  13.3 us
    all_gather x1, blocking collectives, body(): lax.all_gather(defect[None], 'tm', axis=0, tiled=True)  13.1 us
    another operation x1, local copies, waits for them, and re-layouts, restrict(): field.reshape(field.shape[0], field.shape[1] // CF, CF, field.shape[2] //...  6.49 us
    reshape x1, local copies, waits for them, and re-layouts, restrict(): field.reshape(field.shape[0], field.shape[1] // CF, CF, field.shape[2] //...  5.67 us
    reduce_sum x2, other arithmetic, restrict(): return jnp.mean(blocks, axis=(2, 4))  5.09 us
    ppermute x9, starting transfers between devices, padded_2(): lax.ppermute(lax.slice_in_dim(block, block.shape[dim] - width, None, axis...  3.32 us
  transfers between devices with their start and end apart: 18, of which 13 were waited for; matrix products, arithmetic and copies ran while one was open for 23% of the time, Pallas kernels for 0%

commit v1 on v0

--- a/solution.py
+++ b/solution.py
@@ -7,6 +7,28 @@
 CF = 4
 COURANT = 0.06
 DIFFUSION = 0.04
+
+
+def laid_out(blocks, dim):
+    blocks = jnp.moveaxis(blocks, 0, dim)
+    lengths = blocks.shape
+    return blocks.reshape(*lengths[:dim], lengths[dim] * lengths[dim + 1], *lengths[dim + 2 :])
+
+
+def collected_by_bits(shard, axis):
+    size = lax.axis_size(axis)
+    blocks = shard[None]
+    for level in range(size.bit_length() - 1):
+        bit = 1 << level
+        other = lax.ppermute(blocks, axis, [(i, i ^ bit) for i in range(size)])
+        both = jnp.stack([blocks, other])
+        upper = lax.axis_index(axis) >> level & 1
+        blocks = jnp.where(upper == 0, both, both[::-1]).reshape(-1, *shard.shape)
+    return blocks
+
+
+def collect(shard, axis, dim):
+    return laid_out(collected_by_bits(shard, axis), dim)
 
 
 def padded_2(block, sides, width):
@@ -68,7 +90,7 @@
     group_index = lax.axis_index("tm")
     all_start, all_defect = (
         lax.all_gather(start_coarse[None], "tm", axis=0, tiled=True),
-        lax.all_gather(defect[None], "tm", axis=0, tiled=True),
+        collect(defect[None], "tm", 0),
     )
 
     def chain_step(carry, defect_term):

time: 85.1 us -> 78.2 us (0.919)
  blocking collectives: 27.3 us -> 13.1 us
  starting transfers between devices: 16.6 us -> 22.1 us
  waiting for transfers between devices: 17.4 us -> 19 us
    all_gather x1 -> x0, blocking collectives: 13.1 us -> none  [body(): lax.all_gather(defect[None], 'tm', axis=0, tiled=True)]
    ppermute x0 -> x2, starting transfers between devices: none -> 5.49 us  [collected_by_bits(): other = lax.ppermute(blocks, axis, [(i, i ^ bit) for i in range(size)])]
    ppermute x0 -> x2, waiting for transfers between devices: none -> 1.63 us  [collected_by_bits(): other = lax.ppermute(blocks, axis, [(i, i ^ bit) for i in range(size)])]
    all_gather x1, blocking collectives: 14.1 us -> 13.1 us  [body(): lax.all_gather(start_coarse[None], 'tm', axis=0, tiled=True)]
  transfers between devices with their start and end apart: 18 -> 20, of which waited for: 13 -> 15; matrix products, arithmetic and copies ran while one was open for 23% -> 25% of each run, Pallas kernels for 0% -> 0%
where the time goes in v1:
time: 78.2 us; the launch traced here: 77.9 us
  starting transfers between devices  22.1 us (28%)
  waiting for transfers between devices  19 us (24%)
  local copies, waits for them, and re-layouts  16 us (20%)
  blocking collectives  13.1 us (17%)
  other arithmetic  7.1 us (9%)
    ppermute x9, waiting for transfers between devices, padded_2(): lax.ppermute(lax.slice_in_dim(block, block.shape[dim] - width, None, axis...  14.5 us
    all_gather x1, blocking collectives, body(): lax.all_gather(start_coarse[None], 'tm', axis=0, tiled=True)  13.1 us
    ppermute x9, starting transfers between devices, padded_2(): lax.ppermute(lax.slice_in_dim(block, 0, width, axis=dim), axis, backward)  12.5 us
    another operation x1, local copies, waits for them, and re-layouts, restrict(): field.reshape(field.shape[0], field.shape[1] // CF, CF, field.shape[2] //...  6.49 us
    reshape x1, local copies, waits for them, and re-layouts, restrict(): field.reshape(field.shape[0], field.shape[1] // CF, CF, field.shape[2] //...  5.67 us
    ppermute x2, starting transfers between devices, collected_by_bits(): other = lax.ppermute(blocks, axis, [(i, i ^ bit) for i in range(size)])  5.49 us
    reduce_sum x2, other arithmetic, restrict(): return jnp.mean(blocks, axis=(2, 4))  5.09 us
    ppermute x9, starting transfers between devices, padded_2(): lax.ppermute(lax.slice_in_dim(block, block.shape[dim] - width, None, axis...  4.12 us
  transfers between devices with their start and end apart: 20, of which 15 were waited for; matrix products, arithmetic and copies ran while one was open for 25% of the time, Pallas kernels for 0%

profile of v1, /device:TPU:0, one launch (start us, length us, event | category | flops | bytes accessed | tf_op | source)
XLA Modules:
  0.0 77.9 jit_solution(10850575216299611679)
XLA Ops:
  0.0 1.0 %fusion.76 = (f32[2,1,2048]{2,1,0:T(1,128)S(1)}, f32[2,1,2048]{2,1,0:T(1,128)S(1)}) fusion(f32[2,8,2048]{2,1,0:T(8,128)} %bitcast.76), kind=kLoop, calls=%fused_computation.134 | loop fusion | bytes 65536 | tf_op jit(solution)/shard_map/slice | solution.py:41
  1.6 2.9 %collective-permute-start.3 = (f32[2,1,2048]{2,0,1:T(2,128)S(1)}, f32[2,1,2048]{2,0,1:T(2,128)S(1)}, u32[]{:S(2)}, u32[]{:S(2)}) collective-permute-start(f32[2,1,2048]{2,0,1:T(2,128)S(1)} %copy.154), channel_id=1, source_target_pairs={{1,0},{2,1},{3,2},{4,3},{5,4},{6,5},{7,6},{0,7},{9,8},{10,9},{11,1... | collective-permute-start | bytes 49160 | tf_op jit(solution)/shard_map/ppermute | solution.py:43
  4.5 6.5 %reshape_squeeze.3 = f32[2,2,4,512,4]{4,3,2,1,0:T(8,128)} reshape(f32[1,2,8,2048]{3,2,1,0:T(8,128)} %param.3) | data formatting | bytes 262144 | tf_op jit(solution)/shard_map/reshape;squeeze | solution.py:69
  11.0 2.5 %reduce_sum.18 = f32[2,2,512]{2,1,0:T(2,128)S(1)} reduce(f32[2,2,4,512,4]{4,3,2,1,0:T(8,128)} %reshape_squeeze.3, f32[]{:T(128)} %constant.11.clone.1), dimensions={2,4}, to_apply=%region_0.1 | reduce | flops 30720 | bytes 139268 | tf_op jit(solution)/shard_map/reduce_sum | solution.py:70
  13.7 2.6 %collective-permute-start.11 = (f32[2,1,512]{2,1,0:T(1,128)S(1)}, f32[2,1,512]{2,1,0:T(1,128)S(1)}, u32[]{:S(2)}, u32[]{:S(2)}) collective-permute-start(f32[2,1,512]{2,1,0:T(1,128)S(1)} %get-tuple-element.95), channel_id=1, source_target_pairs={{1,0},{2,1},{3,2},{4,3},{5,4},{6,5},{7,6},{0,7},{9,8},{10,9},{11,1... | collective-permute-start | bytes 12296 | tf_op jit(solution)/shard_map/ppermute | solution.py:43
  17.2 2.7 %collective-permute-start.5 = (f32[2,1,2048]{2,0,1:T(2,128)S(1)}, f32[2,1,2048]{2,0,1:T(2,128)S(1)}, u32[]{:S(2)}, u32[]{:S(2)}) collective-permute-start(f32[2,1,2048]{2,0,1:T(2,128)S(1)} %copy.158), channel_id=1, source_target_pairs={{1,0},{2,1},{3,2},{4,3},{5,4},{6,5},{7,6},{0,7},{9,8},{10,9},{11,1... | collective-permute-start | bytes 49160 | tf_op jit(solution)/shard_map/ppermute | solution.py:43
  19.9 1.3 %collective-permute-done.4 = f32[2,1,2048]{2,0,1:T(2,128)S(1)} collective-permute-done((f32[2,1,2048]{2,0,1:T(2,128)S(1)}, f32[2,1,2048]{2,0,1:T(2,128)S(1)}, u32[]{:S(2)}, u32[]{:S(2)}) %collective-permute-start.4) | collective-permute-done | bytes 16416 | tf_op jit(solution)/shard_map/ppermute | solution.py:40
  21.7 2.7 %collective-permute-start.7 = (f32[2,1,2048]{2,0,1:T(2,128)S(1)}, f32[2,1,2048]{2,0,1:T(2,128)S(1)}, u32[]{:S(2)}, u32[]{:S(2)}) collective-permute-start(f32[2,1,2048]{2,0,1:T(2,128)S(1)} %copy.162), channel_id=1, source_target_pairs={{1,0},{2,1},{3,2},{4,3},{5,4},{6,5},{7,6},{0,7},{9,8},{10,9},{11,1... | collective-permute-start | bytes 49160 | tf_op jit(solution)/shard_map/ppermute | solution.py:43
  24.5 1.3 %collective-permute-done.6 = f32[2,1,2048]{2,0,1:T(2,128)S(1)} collective-permute-done((f32[2,1,2048]{2,0,1:T(2,128)S(1)}, f32[2,1,2048]{2,0,1:T(2,128)S(1)}, u32[]{:S(2)}, u32[]{:S(2)}) %collective-permute-start.6) | collective-permute-done | bytes 16416 | tf_op jit(solution)/shard_map/ppermute | solution.py:40
  26.2 1.4 %collective-permute-start.8 = (f32[2,1,2048]{2,0,1:T(2,128)S(1)}, f32[2,1,2048]{2,0,1:T(2,128)S(1)}, u32[]{:S(2)}, u32[]{:S(2)}) collective-permute-start(f32[2,1,2048]{2,0,1:T(2,128)S(1)} %copy.164), channel_id=1, source_target_pairs={{0,1},{1,2},{2,3},{3,4},{4,5},{5,6},{6,7},{7,0},{8,9},{9,10},{10,1... | collective-permute-start | bytes 49160 | tf_op jit(solution)/shard_map/ppermute | solution.py:40
  27.6 1.3 %collective-permute-start.9 = (f32[2,1,2048]{2,0,1:T(2,128)S(1)}, f32[2,1,2048]{2,0,1:T(2,128)S(1)}, u32[]{:S(2)}, u32[]{:S(2)}) collective-permute-start(f32[2,1,2048]{2,0,1:T(2,128)S(1)} %copy.166), channel_id=1, source_target_pairs={{1,0},{2,1},{3,2},{4,3},{5,4},{6,5},{7,6},{0,7},{9,8},{10,9},{11,1... | collective-permute-start | bytes 49160 | tf_op jit(solution)/shard_map/ppermute | solution.py:43
  29.0 1.3 %collective-permute-done.8 = f32[2,1,2048]{2,0,1:T(2,128)S(1)} collective-permute-done((f32[2,1,2048]{2,0,1:T(2,128)S(1)}, f32[2,1,2048]{2,0,1:T(2,128)S(1)}, u32[]{:S(2)}, u32[]{:S(2)}) %collective-permute-start.8) | collective-permute-done | bytes 16416 | tf_op jit(solution)/shard_map/ppermute | solution.py:40
  30.6 5.7 %reshape.59 = f32[2,2,4,512,4]{4,3,2,1,0:T(8,128)} reshape(f32[2,8,2048]{2,1,0:T(8,128)S(1)} %fusion.6) | data formatting | bytes 262144 | tf_op jit(solution)/shard_map/reshape | solution.py:69
  36.3 2.5 %reduce_sum.19 = f32[2,2,512]{2,1,0:T(2,128)S(1)} reduce(f32[2,2,4,512,4]{4,3,2,1,0:T(8,128)} %reshape.59, f32[]{:T(128)} %constant.11.clone.1), dimensions={2,4}, to_apply=%region_1.2 | reduce | flops 30720 | bytes 139268 | tf_op jit(solution)/shard_map/reduce_sum | solution.py:70
  38.9 2.4 %collective-permute-start.12 = (f32[1,1,2,2,512]{4,3,2,1,0:T(2,128)S(1)}, f32[1,1,2,2,512]{4,3,2,1,0:T(2,128)S(1)}, u32[]{:S(2)}, u32[]{:S(2)}) collective-permute-start(f32[1,1,2,2,512]{4,3,2,1,0:T(2,128)S(1)} %bitcast.82), channel_id=1, source_target_pairs={{0,8},{8,0},{16,24},{24,16},{1,9},{9,1},{17,25},{25,17},{2,10},{10... | collective-permute-start | bytes 24584 | tf_op jit(solution)/shard_map/ppermute | solution.py:23
  41.3 1.6 %collective-permute-done.12 = f32[1,1,2,2,512]{4,3,2,1,0:T(2,128)S(1)} collective-permute-done((f32[1,1,2,2,512]{4,3,2,1,0:T(2,128)S(1)}, f32[1,1,2,2,512]{4,3,2,1,0:T(2,128)S(1)}, u32[]{:S(2)}, u32[]{:S(2)}) %collective-permute-start.12) | collective-permute-done | bytes 8224 | tf_op jit(solution)/shard_map/ppermute | solution.py:23
  43.0 3.1 %collective-permute-start.13 = (f32[2,1,2,2,512]{4,3,2,0,1:T(2,128)S(1)}, f32[2,1,2,2,512]{4,3,2,0,1:T(2,128)S(1)}, u32[]{:S(2)}, u32[]{:S(2)}) collective-permute-start(f32[2,1,2,2,512]{4,3,2,0,1:T(2,128)S(1)} %get-tuple-element.89), channel_id=1, source_target_pairs={{0,16},{8,24},{16,0},{24,8},{1,17},{9,25},{17,1},{25,9},{2,18},{10... | collective-permute-start | bytes 49160 | tf_op jit(solution)/shard_map/ppermute | solution.py:23
  46.1 13.1 %all-gather = f32[8,2,512]{2,1,0:T(2,128)S(1)} all-gather(f32[2,2,512]{2,1,0:T(2,128)S(1)} %broadcast_multiply_fusion), channel_id=2, replica_groups=mesh['tm'=4,'space'=8] {'tm'}, dimensions={0}, use_global_device_ids=true | all-gather | bytes 40960 | tf_op jit(solution)/shard_map/all_gather | solution.py:92
  59.3 16.8 %while.12 = (s32[]{:T(128)}, f32[2,2,512]{2,1,0:T(2,128)S(1)}, f32[4,2,2,512]{3,2,1,0:T(2,128)S(1)}, f32[4,2,2,512]{3,2,1,0:T(2,128)S(1)}, s32[]{:T(128)}) while((s32[]{:T(128)}, f32[2,2,512]{2,1,0:T(2,128)S(1)}, f32[4,2,2,512]{3,2,1,0:T(2,128)S(1)}, f32[4,2,2,512]{3,2,1,0:T(2,128)S(1)}, s32[]{:T(128)}) %tuple.69), condition=%wide.region_3.4_spmd, body=%wide.region_2.3_spmd.sunk | while | flops 55298 | bytes 200857 | solution.py:100
  60.7 2.7 %collective-permute-done.1 = f32[2,1,512]{2,1,0:T(1,128)S(1)} collective-permute-done((f32[2,1,512]{2,1,0:T(1,128)S(1)}, f32[2,1,512]{2,1,0:T(1,128)S(1)}, u32[]{:S(2)}, u32[]{:S(2)}) %collective-permute-start.1) | collective-permute-done | bytes 4128 | tf_op jit(solution)/shard_map/while/body/eval_jaxpr/ppermute | solution.py:40
  64.9 2.7 %collective-permute-done.1 = f32[2,1,512]{2,1,0:T(1,128)S(1)} collective-permute-done((f32[2,1,512]{2,1,0:T(1,128)S(1)}, f32[2,1,512]{2,1,0:T(1,128)S(1)}, u32[]{:S(2)}, u32[]{:S(2)}) %collective-permute-start.1) | collective-permute-done | bytes 4128 | tf_op jit(solution)/shard_map/while/body/eval_jaxpr/ppermute | solution.py:40
  69.1 2.7 %collective-permute-done.1 = f32[2,1,512]{2,1,0:T(1,128)S(1)} collective-permute-done((f32[2,1,512]{2,1,0:T(1,128)S(1)}, f32[2,1,512]{2,1,0:T(1,128)S(1)}, u32[]{:S(2)}, u32[]{:S(2)}) %collective-permute-start.1) | collective-permute-done | bytes 4128 | tf_op jit(solution)/shard_map/while/body/eval_jaxpr/ppermute | solution.py:40
  73.3 2.7 %collective-permute-done.1 = f32[2,1,512]{2,1,0:T(1,128)S(1)} collective-permute-done((f32[2,1,512]{2,1,0:T(1,128)S(1)}, f32[2,1,512]{2,1,0:T(1,128)S(1)}, u32[]{:S(2)}, u32[]{:S(2)}) %collective-permute-start.1) | collective-permute-done | bytes 4128 | tf_op jit(solution)/shard_map/while/body/eval_jaxpr/ppermute | solution.py:40
  77.2 0.7 add_bitcast_fusion
  (103 shorter events, 10.0 us)
Async XLA Ops:
  1.0 15.6 %collective-permute-start.2 = (f32[2,1,2048]{2,0,1:T(2,128)S(1)}, f32[2,1,2048]{2,0,1:T(2,128)S(1)}, u32[]{:S(2)}, u32[]{:S(2)}) collective-permute-start(f32[2,1,2048]{2,0,1:T(2,128)S(1)} %copy.152), channel_id=1, source_target_pairs={{0,1},{1,2},{2,3},{3,4},{4,5},{5,6},{6,7},{7,0},{8,9},{9,10},{10,1... | collective-permute-start | bytes 49160 | tf_op jit(solution)/shard_map/ppermute | solution.py:40
  1.6 14.7 %copy-start = (f32[1,2,8,2048]{3,2,1,0:T(8,128)S(1)}, f32[1,2,8,2048]{3,2,1,0:T(8,128)}, u32[]{:S(2)}) copy-start(f32[1,2,8,2048]{3,2,1,0:T(8,128)} %param.3) | copy-start | bytes 393220
  1.6 15.1 %collective-permute-start.3 = (f32[2,1,2048]{2,0,1:T(2,128)S(1)}, f32[2,1,2048]{2,0,1:T(2,128)S(1)}, u32[]{:S(2)}, u32[]{:S(2)}) collective-permute-start(f32[2,1,2048]{2,0,1:T(2,128)S(1)} %copy.154), channel_id=1, source_target_pairs={{1,0},{2,1},{3,2},{4,3},{5,4},{6,5},{7,6},{0,7},{9,8},{10,9},{11,1... | collective-permute-start | bytes 49160 | tf_op jit(solution)/shard_map/ppermute | solution.py:43
  13.6 25.2 %collective-permute-start.10 = (f32[2,1,512]{2,1,0:T(1,128)S(1)}, f32[2,1,512]{2,1,0:T(1,128)S(1)}, u32[]{:S(2)}, u32[]{:S(2)}) collective-permute-start(f32[2,1,512]{2,1,0:T(1,128)S(1)} %get-tuple-element.94), channel_id=1, source_target_pairs={{0,1},{1,2},{2,3},{3,4},{4,5},{5,6},{6,7},{7,0},{8,9},{9,10},{10,1... | collective-permute-start | bytes 12296 | tf_op jit(solution)/shard_map/ppermute | solution.py:40
  13.7 25.2 %collective-permute-start.11 = (f32[2,1,512]{2,1,0:T(1,128)S(1)}, f32[2,1,512]{2,1,0:T(1,128)S(1)}, u32[]{:S(2)}, u32[]{:S(2)}) collective-permute-start(f32[2,1,512]{2,1,0:T(1,128)S(1)} %get-tuple-element.95), channel_id=1, source_target_pairs={{1,0},{2,1},{3,2},{4,3},{5,4},{6,5},{7,6},{0,7},{9,8},{10,9},{11,1... | collective-permute-start | bytes 12296 | tf_op jit(solution)/shard_map/ppermute | solution.py:43
  17.1 4.1 %collective-permute-start.4 = (f32[2,1,2048]{2,0,1:T(2,128)S(1)}, f32[2,1,2048]{2,0,1:T(2,128)S(1)}, u32[]{:S(2)}, u32[]{:S(2)}) collective-permute-start(f32[2,1,2048]{2,0,1:T(2,128)S(1)} %copy.156), channel_id=1, source_target_pairs={{0,1},{1,2},{2,3},{3,4},{4,5},{5,6},{6,7},{7,0},{8,9},{9,10},{10,1... | collective-permute-start | bytes 49160 | tf_op jit(solution)/shard_map/ppermute | solution.py:40
  17.2 4.1 %collective-permute-start.5 = (f32[2,1,2048]{2,0,1:T(2,128)S(1)}, f32[2,1,2048]{2,0,1:T(2,128)S(1)}, u32[]{:S(2)}, u32[]{:S(2)}) collective-permute-start(f32[2,1,2048]{2,0,1:T(2,128)S(1)} %copy.158), channel_id=1, source_target_pairs={{1,0},{2,1},{3,2},{4,3},{5,4},{6,5},{7,6},{0,7},{9,8},{10,9},{11,1... | collective-permute-start | bytes 49160 | tf_op jit(solution)/shard_map/ppermute | solution.py:43
  21.6 4.1 %collective-permute-start.6 = (f32[2,1,2048]{2,0,1:T(2,128)S(1)}, f32[2,1,2048]{2,0,1:T(2,128)S(1)}, u32[]{:S(2)}, u32[]{:S(2)}) collective-permute-start(f32[2,1,2048]{2,0,1:T(2,128)S(1)} %copy.160), channel_id=1, source_target_pairs={{0,1},{1,2},{2,3},{3,4},{4,5},{5,6},{6,7},{7,0},{8,9},{9,10},{10,1... | collective-permute-start | bytes 49160 | tf_op jit(solution)/shard_map/ppermute | solution.py:40
  21.7 4.1 %collective-permute-start.7 = (f32[2,1,2048]{2,0,1:T(2,128)S(1)}, f32[2,1,2048]{2,0,1:T(2,128)S(1)}, u32[]{:S(2)}, u32[]{:S(2)}) collective-permute-start(f32[2,1,2048]{2,0,1:T(2,128)S(1)} %copy.162), channel_id=1, source_target_pairs={{1,0},{2,1},{3,2},{4,3},{5,4},{6,5},{7,6},{0,7},{9,8},{10,9},{11,1... | collective-permute-start | bytes 49160 | tf_op jit(solution)/shard_map/ppermute | solution.py:43
  26.2 4.1 %collective-permute-start.8 = (f32[2,1,2048]{2,0,1:T(2,128)S(1)}, f32[2,1,2048]{2,0,1:T(2,128)S(1)}, u32[]{:S(2)}, u32[]{:S(2)}) collective-permute-start(f32[2,1,2048]{2,0,1:T(2,128)S(1)} %copy.164), channel_id=1, source_target_pairs={{0,1},{1,2},{2,3},{3,4},{4,5},{5,6},{6,7},{7,0},{8,9},{9,10},{10,1... | collective-permute-start | bytes 49160 | tf_op jit(solution)/shard_map/ppermute | solution.py:40
  27.6 2.8 %collective-permute-start.9 = (f32[2,1,2048]{2,0,1:T(2,128)S(1)}, f32[2,1,2048]{2,0,1:T(2,128)S(1)}, u32[]{:S(2)}, u32[]{:S(2)}) collective-permute-start(f32[2,1,2048]{2,0,1:T(2,128)S(1)} %copy.166), channel_id=1, source_target_pairs={{1,0},{2,1},{3,2},{4,3},{5,4},{6,5},{7,6},{0,7},{9,8},{10,9},{11,1... | collective-permute-start | bytes 49160 | tf_op jit(solution)/shard_map/ppermute | solution.py:43
  38.9 4.0 %collective-permute-start.12 = (f32[1,1,2,2,512]{4,3,2,1,0:T(2,128)S(1)}, f32[1,1,2,2,512]{4,3,2,1,0:T(2,128)S(1)}, u32[]{:S(2)}, u32[]{:S(2)}) collective-permute-start(f32[1,1,2,2,512]{4,3,2,1,0:T(2,128)S(1)} %bitcast.82), channel_id=1, source_target_pairs={{0,8},{8,0},{16,24},{24,16},{1,9},{9,1},{17,25},{25,17},{2,10},{10... | collective-permute-start | bytes 24584 | tf_op jit(solution)/shard_map/ppermute | solution.py:23
  43.0 16.2 %collective-permute-start.13 = (f32[2,1,2,2,512]{4,3,2,0,1:T(2,128)S(1)}, f32[2,1,2,2,512]{4,3,2,0,1:T(2,128)S(1)}, u32[]{:S(2)}, u32[]{:S(2)}) collective-permute-start(f32[2,1,2,2,512]{4,3,2,0,1:T(2,128)S(1)} %get-tuple-element.89), channel_id=1, source_target_pairs={{0,16},{8,24},{16,0},{24,8},{1,17},{9,25},{17,1},{25,9},{2,18},{10... | collective-permute-start | bytes 49160 | tf_op jit(solution)/shard_map/ppermute | solution.py:23
  59.3 1.4 %collective-permute-start = (f32[2,1,512]{2,1,0:T(1,128)S(1)}, f32[2,1,512]{2,1,0:T(1,128)S(1)}, u32[]{:S(2)}, u32[]{:S(2)}) collective-permute-start(f32[2,1,512]{2,1,0:T(1,128)S(1)} %get-tuple-element.143), channel_id=1, source_target_pairs={{1,0},{2,1},{3,2},{4,3},{5,4},{6,5},{7,6},{0,7},{9,8},{10,9},{11,1... | collective-permute-start | bytes 12296 | tf_op jit(solution)/shard_map/while/body/eval_jaxpr/ppermute | solution.py:43
  59.4 4.0 %collective-permute-start.1 = (f32[2,1,512]{2,1,0:T(1,128)S(1)}, f32[2,1,512]{2,1,0:T(1,128)S(1)}, u32[]{:S(2)}, u32[]{:S(2)}) collective-permute-start(f32[2,1,512]{2,1,0:T(1,128)S(1)} %get-tuple-element.145), channel_id=1, source_target_pairs={{0,1},{1,2},{2,3},{3,4},{4,5},{5,6},{6,7},{7,0},{8,9},{9,10},{10,1... | collective-permute-start | bytes 12296 | tf_op jit(solution)/shard_map/while/body/eval_jaxpr/ppermute | solution.py:40
  63.5 1.4 %collective-permute-start = (f32[2,1,512]{2,1,0:T(1,128)S(1)}, f32[2,1,512]{2,1,0:T(1,128)S(1)}, u32[]{:S(2)}, u32[]{:S(2)}) collective-permute-start(f32[2,1,512]{2,1,0:T(1,128)S(1)} %get-tuple-element.143), channel_id=1, source_target_pairs={{1,0},{2,1},{3,2},{4,3},{5,4},{6,5},{7,6},{0,7},{9,8},{10,9},{11,1... | collective-permute-start | bytes 12296 | tf_op jit(solution)/shard_map/while/body/eval_jaxpr/ppermute | solution.py:43
  63.6 4.0 %collective-permute-start.1 = (f32[2,1,512]{2,1,0:T(1,128)S(1)}, f32[2,1,512]{2,1,0:T(1,128)S(1)}, u32[]{:S(2)}, u32[]{:S(2)}) collective-permute-start(f32[2,1,512]{2,1,0:T(1,128)S(1)} %get-tuple-element.145), channel_id=1, source_target_pairs={{0,1},{1,2},{2,3},{3,4},{4,5},{5,6},{6,7},{7,0},{8,9},{9,10},{10,1... | collective-permute-start | bytes 12296 | tf_op jit(solution)/shard_map/while/body/eval_jaxpr/ppermute | solution.py:40
  67.7 1.4 %collective-permute-start = (f32[2,1,512]{2,1,0:T(1,128)S(1)}, f32[2,1,512]{2,1,0:T(1,128)S(1)}, u32[]{:S(2)}, u32[]{:S(2)}) collective-permute-start(f32[2,1,512]{2,1,0:T(1,128)S(1)} %get-tuple-element.143), channel_id=1, source_target_pairs={{1,0},{2,1},{3,2},{4,3},{5,4},{6,5},{7,6},{0,7},{9,8},{10,9},{11,1... | collective-permute-start | bytes 12296 | tf_op jit(solution)/shard_map/while/body/eval_jaxpr/ppermute | solution.py:43
  67.7 4.0 %collective-permute-start.1 = (f32[2,1,512]{2,1,0:T(1,128)S(1)}, f32[2,1,512]{2,1,0:T(1,128)S(1)}, u32[]{:S(2)}, u32[]{:S(2)}) collective-permute-start(f32[2,1,512]{2,1,0:T(1,128)S(1)} %get-tuple-element.145), channel_id=1, source_target_pairs={{0,1},{1,2},{2,3},{3,4},{4,5},{5,6},{6,7},{7,0},{8,9},{9,10},{10,1... | collective-permute-start | bytes 12296 | tf_op jit(solution)/shard_map/while/body/eval_jaxpr/ppermute | solution.py:40
  71.9 1.4 %collective-permute-start = (f32[2,1,512]{2,1,0:T(1,128)S(1)}, f32[2,1,512]{2,1,0:T(1,128)S(1)}, u32[]{:S(2)}, u32[]{:S(2)}) collective-permute-start(f32[2,1,512]{2,1,0:T(1,128)S(1)} %get-tuple-element.143), channel_id=1, source_target_pairs={{1,0},{2,1},{3,2},{4,3},{5,4},{6,5},{7,6},{0,7},{9,8},{10,9},{11,1... | collective-permute-start | bytes 12296 | tf_op jit(solution)/shard_map/while/body/eval_jaxpr/ppermute | solution.py:43
  71.9 4.0 %collective-permute-start.1 = (f32[2,1,512]{2,1,0:T(1,128)S(1)}, f32[2,1,512]{2,1,0:T(1,128)S(1)}, u32[]{:S(2)}, u32[]{:S(2)}) collective-permute-start(f32[2,1,512]{2,1,0:T(1,128)S(1)} %get-tuple-element.145), channel_id=1, source_target_pairs={{0,1},{1,2},{2,3},{3,4},{4,5},{5,6},{6,7},{7,0},{8,9},{9,10},{10,1... | collective-permute-start | bytes 12296 | tf_op jit(solution)/shard_map/while/body/eval_jaxpr/ppermute | solution.py:40
